TPU v7x, 32 devices: a whole 2x2x4 slice. The times are simulated.
32 devices in a mesh: groups: 2 (over x), dp: 16 (over z, y, core).
Axes of the slice: x: 2, y: 2, z: 4, core: 2. Of those that a mesh axis runs over, the one named last changes fastest.
Arguments:
- inputs: bfloat16 [64, 128, 4096], P(('groups', 'dp')), parts along dimension 0, may hold values from -6 to 6
- outputs: bfloat16 [64, 128, 4096], P(('groups', 'dp')), parts along dimension 0, may hold values from -6 to 6
- lengths: int32 [64], P(('groups', 'dp')), parts along dimension 0, may hold values from 64 to 128
- labels: int32 [64], P(('groups', 'dp')), parts along dimension 0, may hold values from 0 to 13
- norm_gain: float32 [4096], replicated, may hold values from 0.1 to 1.9
- classifier: bfloat16 [4096, 14], replicated, may hold values from -0.09375 to 0.09375
- proj_in: bfloat16 [4096, 64], replicated, may hold values from -0.09375 to 0.09375
- proj_out: bfloat16 [4096, 128], replicated, may hold values from -0.09375 to 0.09375
- query_index: int32 [256], P('groups'), parts along dimension 0, may hold values from 0 to 31, as said below
- prior_fisher: float32 [16384, 8192], P('groups', 'dp'), parts along dimension 0, may hold values from -4 to 18, as said below
Outputs:
- influence: float32 [8192, 256], P('dp', 'groups'), parts along dimension 1
- scores: float32 [64, 128], P(('groups', 'dp')), parts along dimension 0
There are 2 independent parts, one for each index of `groups`. A program takes and returns all parts, laid end to end along the dimension named above; an argument that names none is the same for every part. Nothing has to cross between parts.
Inputs may be any that keep to these rules, and one draw needn't show every extreme that they name: `query_index`: indices may repeat. `prior_fisher`: symmetric and positive definite.
All inputs are finite; a program needn't handle non-finite values.
Results may differ from a plain program's by a relative error of at most 0.0044.
Values may be sent and summed in bfloat16 or wider, within the bound.
A program may use at most 128 MiB of HBM per device.

v0:
```python
import jax
import jax.numpy as jnp
from jax import lax
from jax.sharding import PartitionSpec as P

D = 4096
CLASSES = 14
ITERS = 4
norm_eps = 1e-05
damp_share = 0.5
highest = lax.Precision.HIGHEST


def project_rows(inputs, outputs, lengths, labels, norm_gain, classifier, proj_in, proj_out):
    ex_count = inputs.shape[0]
    tok_count = inputs.shape[1]
    hidden = outputs.astype(jnp.float32)
    root_mean = jnp.sqrt(jnp.mean(hidden * hidden, axis=-1, keepdims=True) + norm_eps)
    positions = jnp.arange(tok_count, dtype=jnp.int32)
    live_mask = (positions[None, :] < lengths[:, None]).astype(jnp.float32)[:, :, None]
    length_float = lengths.astype(jnp.float32)[:, None, None]
    normed = norm_gain * hidden / root_mean
    pooled = jnp.sum(live_mask * normed, axis=1) / length_float[:, 0]
    class_weight = classifier.astype(jnp.float32)
    logits = jnp.dot(pooled, class_weight, precision=highest)
    exponent = jnp.exp(logits)
    probs = exponent / jnp.sum(exponent, axis=-1, keepdims=True)
    target = (jnp.arange(CLASSES, dtype=jnp.int32)[None, :] == labels[:, None]).astype(jnp.float32)
    pooled_grad = lax.dot_general(
        probs - target, class_weight, (((1,), (1,)), ((), ())), precision=highest
    )
    scaled = norm_gain * (live_mask / length_float) * pooled_grad[:, None, :]
    out_grad = scaled / root_mean - hidden * jnp.sum(hidden * scaled, axis=-1, keepdims=True) / (
        D * root_mean**3
    )
    grad_low = out_grad.astype(jnp.bfloat16)
    input_proj = jnp.dot(
        inputs.reshape(ex_count * tok_count, D).astype(jnp.float32),
        proj_in.astype(jnp.float32),
        precision=highest,
    )
    grad_proj = jnp.dot(
        grad_low.reshape(ex_count * tok_count, D).astype(jnp.float32),
        proj_out.astype(jnp.float32),
        precision=highest,
    )
    input_proj = input_proj.reshape(ex_count, tok_count, -1)
    grad_proj = grad_proj.reshape(ex_count, tok_count, -1)
    outer = jnp.einsum("eta,etb->eab", input_proj, grad_proj, precision=highest)
    return outer.reshape(ex_count, -1).astype(jnp.bfloat16)


def conjugate(queries, apply_fisher, reduce_inner):
    solved = jnp.zeros_like(queries)
    residual = queries
    direction = queries
    norm_now = reduce_inner(residual, residual)
    for step_index in range(ITERS):
        image = apply_fisher(direction)
        alpha = norm_now / reduce_inner(direction, image)
        solved = solved + alpha * direction
        residual = residual - alpha * image
        norm_next = reduce_inner(residual, residual)
        direction = residual + norm_next / norm_now * direction
        norm_now = norm_next
    return solved


def pieces_inner(first_vec, second_vec):
    return lax.psum(jnp.sum(first_vec * second_vec, axis=0), "dp")


def contract_rows(left_rows, right_rows):
    return jnp.dot(
        left_rows.astype(jnp.float32).T, right_rows.astype(jnp.float32), precision=highest
    )


def body(
    inputs,
    outputs,
    lengths,
    labels,
    norm_gain,
    classifier,
    proj_in,
    proj_out,
    query_index,
    prior_fisher,
):
    own_rows = project_rows(
        inputs, outputs, lengths, labels, norm_gain, classifier, proj_in, proj_out
    )
    devices = lax.axis_size("dp")
    device_index = lax.axis_index("dp")
    own_count = own_rows.shape[0]
    total_rows = own_count * devices
    width = own_rows.shape[1]
    piece = width // devices
    own_float = own_rows.astype(jnp.float32)
    square_sum = lax.psum(jnp.sum(own_float * own_float), "dp")
    damping = damp_share * square_sum / (total_rows * total_rows)
    every = lax.all_gather(own_rows, "dp", axis=0, tiled=True)
    mine = lax.dynamic_slice_in_dim(every, device_index * piece, piece, 1)
    strip = contract_rows(every, mine) / total_rows + damping * prior_fisher

    def apply_piece(vectors):
        return lax.psum_scatter(
            jnp.dot(strip, vectors, precision=highest), "dp", scatter_dimension=0, tiled=True
        )

    queries = jnp.take(mine, query_index, axis=0).astype(jnp.float32).T
    solved = conjugate(queries, apply_piece, pieces_inner)
    block = mine.astype(jnp.float32)
    scores = lax.psum_scatter(
        jnp.dot(block, solved, precision=highest) / total_rows,
        "dp",
        scatter_dimension=0,
        tiled=True,
    )
    return (solved, scores)


def solution(mesh):
    return jax.shard_map(
        body,
        mesh=mesh,
        in_specs=(
            P(("groups", "dp"), None, None),
            P(("groups", "dp"), None, None),
            P(("groups", "dp")),
            P(("groups", "dp")),
            P(),
            P(),
            P(),
            P(),
            P("groups"),
            P("groups", "dp"),
        ),
        out_specs=(P("dp", "groups"), P(("groups", "dp"), None)),
        check_vma=False,
    )
```

profile of v0, /device:TPU:0, one launch (start us, length us, event | category | flops | bytes accessed | tf_op | source)
XLA Modules:
  0.0 715.0 jit_solution(6194514816210829395)
XLA Ops:
  10.2 2.1 fusion.6
  13.1 2.5 fusion.8
  16.3 2.1 fusion.3
  19.9 0.8 multiply_reduce_fusion.6
  20.8 24.6 %all-gather = bf16[16,2,8192]{2,1,0:T(2,128)(2,1)S(1)} all-gather(bf16[1,2,8192]{2,1,0:T(2,128)(2,1)S(1)} %reshape.115), channel_id=1, replica_groups=mesh['groups'=2,'dp'=16] {'dp'}, dimensions={0}, use_global_device_ids=true | all-gather | bytes 557056 | tf_op jit(solution)/shard_map/all_gather | solution.py:103
  45.6 30.5 %psum.64 = f32[]{:T(128)} all-reduce(f32[]{:T(128)} %get-tuple-element.12), channel_id=1, replica_groups=mesh['groups'=2,'dp'=16] {'dp'}, use_global_device_ids=true, to_apply=%region_7.8 | all-reduce | flops 1 | bytes 8 | tf_op jit(solution)/shard_map/psum | solution.py:101
  77.7 8.1 %multiply_add_fusion = f32[8192,512]{1,0:T(8,128)S(1)} fusion(f32[8192,512]{1,0:T(8,128)} %param.19, bf16[32,8192]{1,0:T(8,128)(2,1)S(1)} %reshape.116, bf16[32,512]{1,0:T(8,128)(2,1)S(1)} %constant_dynamic-slice_fusion.1, f32[]{:T(128)S(6)} %div.104), kind=kOutput, calls=%fused_computation.2 | convolution fusion | flops 281018368 | bytes 34111492 | tf_op jit(solution)/shard_map/dot_general | solution.py:74
  85.9 5.7 copy-done.1
  91.6 9.1 %fusion.22 = f32[8192,128]{1,0:T(8,128)} fusion(f32[8192,512]{1,0:T(8,128)S(1)} %multiply_add_fusion, bf16[128,512]{0,1:T(8,128)(2,1)S(1)} %copy.13, pred[128]{0:T(512)(128)(4,1)S(1)} %compare_and_fusion), kind=kOutput, calls=%fused_computation.49 | convolution fusion | flops 6442516480 | bytes 21102720 | tf_op jit(solution)/shard_map/dot_general | solution.py:109
  100.7 69.7 %reduce-scatter.5.cloned.1.call-done = f32[512,128]{1,0:T(8,128)} async-done(((f32[8192,128]{1,0:T(8,128)}), f32[512,128]{1,0:T(8,128)}) %reduce-scatter.5.cloned.1.call-update) | async-done | bytes 262160 | tf_op jit(solution)/shard_map/reduce_scatter | solution.py:108
  170.5 1.0 fusion.17
  171.5 30.4 %all-reduce.1 = (f32[128]{0:T(128)S(1)}, f32[128]{0:T(128)S(1)}) all-reduce(f32[128]{0:T(128)S(1)} %get-tuple-element.3, f32[128]{0:T(128)S(1)} %get-tuple-element.2), channel_id=1, replica_groups=mesh['groups'=2,'dp'=16] {'dp'}, use_global_device_ids=true, to_apply=%region_5.0 | all-reduce | flops 256 | bytes 2048 | tf_op jit(solution)/shard_map/psum | solution.py:70
  201.9 1.0 multiply_reduce_fusion.5
  202.9 29.5 %psum.66 = f32[128]{0:T(128)S(1)} all-reduce(f32[128]{0:T(128)S(1)} %multiply_reduce_fusion.5), channel_id=1, replica_groups=mesh['groups'=2,'dp'=16] {'dp'}, use_global_device_ids=true, to_apply=%region_12.13 | all-reduce | flops 128 | bytes 1024 | tf_op jit(solution)/shard_map/psum | solution.py:70
  232.4 17.4 %fusion.31 = f32[8192,128]{1,0:T(8,128)} fusion(f32[8192,512]{1,0:T(8,128)} %copy-done.1, f32[512,128]{1,0:T(8,128)} %reduce-scatter.5.cloned.1.call-done, f32[128]{0:T(128)S(1)} %div.106, f32[128]{0:T(128)S(1)} %div.105, bf16[128,512]{0,1:T(8,128)(2,1)S(1)} %copy.13, pred[128]{0:T(512)(128)(4,1)S(1)} %compare_and_fusion), kind=kOutput, calls=%fused_computation.69 | convolution fusion | flops 6442844160 | bytes 21365888 | tf_op jit(solution)/shard_map/dot_general | solution.py:109
  249.9 69.6 %reduce-scatter.7.cloned.1.call-done = f32[512,128]{1,0:T(8,128)} async-done(((f32[8192,128]{1,0:T(8,128)}), f32[512,128]{1,0:T(8,128)}) %reduce-scatter.7.cloned.1.call-update) | async-done | bytes 262160 | tf_op jit(solution)/shard_map/reduce_scatter | solution.py:108
  319.5 1.0 multiply_reduce_fusion.4
  320.6 30.1 %psum.67 = f32[128]{0:T(128)S(1)} all-reduce(f32[128]{0:T(128)S(1)} %multiply_reduce_fusion.4), channel_id=1, replica_groups=mesh['groups'=2,'dp'=16] {'dp'}, use_global_device_ids=true, to_apply=%region_15.16 | all-reduce | flops 128 | bytes 1024 | tf_op jit(solution)/shard_map/psum | solution.py:70
  350.7 1.0 multiply_reduce_fusion.3
  351.8 29.5 %psum.68 = f32[128]{0:T(128)S(1)} all-reduce(f32[128]{0:T(128)S(1)} %get-tuple-element.6), channel_id=1, replica_groups=mesh['groups'=2,'dp'=16] {'dp'}, use_global_device_ids=true, to_apply=%region_17.18 | all-reduce | flops 128 | bytes 1024 | tf_op jit(solution)/shard_map/psum | solution.py:70
  381.4 17.4 %fusion.34 = f32[8192,128]{1,0:T(8,128)} fusion(f32[8192,512]{1,0:T(8,128)} %copy-done.1, f32[512,128]{1,0:T(8,128)S(1)} %multiply_add_fusion.2), kind=kOutput, calls=%fused_computation.71 | convolution fusion | flops 6442450944 | bytes 21233664 | tf_op jit(solution)/shard_map/dot_general | solution.py:109
  398.8 69.7 %reduce-scatter.9.cloned.1.call-done = f32[512,128]{1,0:T(8,128)} async-done(((f32[8192,128]{1,0:T(8,128)}), f32[512,128]{1,0:T(8,128)}) %reduce-scatter.9.cloned.1.call-update) | async-done | bytes 262160 | tf_op jit(solution)/shard_map/reduce_scatter | solution.py:108
  468.6 1.0 multiply_reduce_fusion.2
  469.6 30.1 %psum.69 = f32[128]{0:T(128)S(1)} all-reduce(f32[128]{0:T(128)S(1)} %multiply_reduce_fusion.2), channel_id=1, replica_groups=mesh['groups'=2,'dp'=16] {'dp'}, use_global_device_ids=true, to_apply=%region_20.21 | all-reduce | flops 128 | bytes 1024 | tf_op jit(solution)/shard_map/psum | solution.py:70
  499.7 1.0 multiply_reduce_fusion.1
  500.8 29.7 %psum.70 = f32[128]{0:T(128)S(1)} all-reduce(f32[128]{0:T(128)S(1)} %multiply_reduce_fusion.1), channel_id=1, replica_groups=mesh['groups'=2,'dp'=16] {'dp'}, use_global_device_ids=true, to_apply=%region_22.23 | all-reduce | flops 128 | bytes 1024 | tf_op jit(solution)/shard_map/psum | solution.py:70
  530.5 1.0 multiply_add_fusion.1
  531.5 17.4 %fusion.35 = f32[8192,128]{1,0:T(8,128)} fusion(f32[8192,512]{1,0:T(8,128)} %copy-done.1, f32[512,128]{1,0:T(8,128)S(1)} %multiply_add_fusion.1), kind=kOutput, calls=%fused_computation.72 | convolution fusion | flops 6442450944 | bytes 21233664 | tf_op jit(solution)/shard_map/dot_general | solution.py:109
  550.8 68.0 %reduce-scatter.11.cloned.1.call-done = f32[512,128]{1,0:T(8,128)} async-done(((f32[8192,128]{1,0:T(8,128)}), f32[512,128]{1,0:T(8,128)}) %reduce-scatter.11.cloned.1.call-update) | async-done | bytes 262160 | tf_op jit(solution)/shard_map/reduce_scatter | solution.py:108
  618.8 1.0 multiply_reduce_fusion
  619.9 30.1 %psum.71 = f32[128]{0:T(128)S(1)} all-reduce(f32[128]{0:T(128)S(1)} %multiply_reduce_fusion), channel_id=1, replica_groups=mesh['groups'=2,'dp'=16] {'dp'}, use_global_device_ids=true, to_apply=%region_25.26 | all-reduce | flops 128 | bytes 1024 | tf_op jit(solution)/shard_map/psum | solution.py:70
  650.3 57.6 %all-reduce = f32[32,128]{1,0:T(8,128)S(1)} all-reduce(f32[32,128]{1,0:T(8,128)S(1)} %convolution_multiply_fusion), channel_id=6, replica_groups=mesh['groups'=2,'dp'=16] {'dp'}, use_global_device_ids=true, to_apply=%region_26.27.clone | all-reduce | flops 4096 | bytes 32768
  (56 shorter events, 9.6 us)
Async XLA Ops:
  7.2 12.0 %copy-start = (bf16[2,128,4096]{2,1,0:T(8,128)(2,1)S(1)}, bf16[2,128,4096]{2,1,0:T(8,128)(2,1)}, u32[]{:S(2)}) copy-start(bf16[2,128,4096]{2,1,0:T(8,128)(2,1)} %param.10) | copy-start | bytes 6291460
  7.2 9.1 %copy-start.7 = (f32[4096]{0:T(1024)S(1)}, f32[4096]{0:T(1024)}, u32[]{:S(2)}) copy-start(f32[4096]{0:T(1024)} %param.14) | copy-start | bytes 49156
  7.2 8.4 %copy-start.8 = (bf16[4096,14]{0,1:T(8,128)(2,1)S(1)}, bf16[4096,14]{0,1:T(8,128)(2,1)}, u32[]{:S(2)}) copy-start(bf16[4096,14]{0,1:T(8,128)(2,1)} %param.15) | copy-start | bytes 344068
  7.2 8.8 %copy-start.9 = (s32[2]{0:T(128)S(1)}, s32[2]{0:T(128)}, u32[]{:S(2)}) copy-start(s32[2]{0:T(128)} %param.13) | copy-start | bytes 28
  7.2 163.2 %reduce-scatter.5.cloned.1.call-start = ((), (), s32[]{:S(2)}) async-start(), calls=%async_computation.4 | async-start | bytes 4456448 | tf_op jit(solution)/shard_map/reduce_scatter | solution.py:108
  7.3 9.1 %copy-start.3 = (bf16[2,128,4096]{2,1,0:T(8,128)(2,1)S(1)}, bf16[2,128,4096]{2,1,0:T(8,128)(2,1)}, u32[]{:S(2)}) copy-start(bf16[2,128,4096]{2,1,0:T(8,128)(2,1)} %param.11) | copy-start | bytes 6291460
  16.3 2.1 copy-start.4
  16.3 2.8 copy-start.6
  85.8 5.7 copy-start.1
  100.7 218.9 %reduce-scatter.7.cloned.1.call-start = ((), (), s32[]{:S(2)}) async-start(), calls=%async_computation.5 | async-start | bytes 4456448 | tf_op jit(solution)/shard_map/reduce_scatter | solution.py:108
  249.8 69.7 %copy-start.2 = (f32[512,128]{1,0:T(8,128)S(1)}, f32[512,128]{1,0:T(8,128)}, u32[]{:S(2)}) copy-start(f32[512,128]{1,0:T(8,128)} %reduce-scatter.5.cloned.1.call-done) | copy-start | bytes 786436
  249.8 218.7 %reduce-scatter.9.cloned.1.call-start = ((), (), s32[]{:S(2)}) async-start(), calls=%async_computation.6 | async-start | bytes 4456448 | tf_op jit(solution)/shard_map/reduce_scatter | solution.py:108
  398.8 220.0 %reduce-scatter.11.cloned.1.call-start = ((), (), s32[]{:S(2)}) async-start(), calls=%async_computation.7 | async-start | bytes 4456448 | tf_op jit(solution)/shard_map/reduce_scatter | solution.py:108
  548.9 0.7 copy-start.10
  650.0 58.4 %copy-start.5 = (f32[512,128]{1,0:T(8,128)}, f32[512,128]{1,0:T(8,128)S(1)}, u32[]{:S(2)}) copy-start(f32[512,128]{1,0:T(8,128)S(1)} %fusion.20) | copy-start | bytes 786436
Sparse Core Ops, SparseCore 0:
  100.8 69.6 reduce-scatter.4
  250.0 69.5 reduce-scatter.6
  398.9 69.6 reduce-scatter.8
  549.1 69.7 reduce-scatter.10
where the time goes:
time: 716 us; the launch traced here: 715 us
  blocking collectives  322 us (45%)
  waiting for transfers between devices  277 us (39%)
  matrix products  72.7 us (10%)
  other arithmetic  18.8 us (3%)
  between operations  15.3 us (2%)
  local copies, waits for them, and re-layouts  8.71 us (1%)
    reduce_scatter x4, waiting for transfers between devices, apply_piece(): lax.psum_scatter(jnp.dot(strip, vectors, precision=highest), 'dp', scatte...  277 us
    psum x7, blocking collectives, pieces_inner(): return lax.psum(jnp.sum(first_vec * second_vec, axis=0), 'dp')  209 us
    dot_general x4, matrix products, apply_piece(): jnp.dot(strip, vectors, precision=highest)  61.4 us
    unnamed x1, blocking collectives  57.6 us
    psum x1, blocking collectives, body(): square_sum = lax.psum(jnp.sum(own_float * own_float), 'dp')  30.5 us
    all_gather x1, blocking collectives, body(): every = lax.all_gather(own_rows, 'dp', axis=0, tiled=True)  24.6 us
  transfers between devices with their start and end apart: 4, of which 4 were waited for; matrix products, arithmetic and copies ran while one was open for 0% of the time, Pallas kernels for 0%

commit v1 on v0

--- a/solution.py
+++ b/solution.py
@@ -67,7 +67,7 @@
 
 
 def pieces_inner(first_vec, second_vec):
-    return lax.psum(jnp.sum(first_vec * second_vec, axis=0), "dp")
+    return jnp.sum(lax.all_gather(jnp.sum(first_vec * second_vec, axis=0), "dp"), axis=0)
 
 
 def contract_rows(left_rows, right_rows):

time: 716 us -> 657 us (0.918)
  blocking collectives: 322 us -> 260 us
    psum x7 -> x0, blocking collectives: 209 us -> none  [pieces_inner(): return lax.psum(jnp.sum(first_vec * second_vec, axis=0), 'dp')]
    all_gather x0 -> x8, blocking collectives: none -> 147 us  [pieces_inner(): lax.all_gather(jnp.sum(first_vec * second_vec, axis=0), 'dp')]
where the time goes in v1:
time: 657 us; the launch traced here: 656 us
  waiting for transfers between devices  280 us (43%)
  blocking collectives  260 us (40%)
  matrix products  72.7 us (11%)
  other arithmetic  19.1 us (3%)
  between operations  15.3 us (2%)
  local copies, waits for them, and re-layouts  8.71 us (1%)
    reduce_scatter x4, waiting for transfers between devices, apply_piece(): lax.psum_scatter(jnp.dot(strip, vectors, precision=highest), 'dp', scatte...  280 us
    all_gather x8, blocking collectives, pieces_inner(): lax.all_gather(jnp.sum(first_vec * second_vec, axis=0), 'dp')  147 us
    dot_general x4, matrix products, apply_piece(): jnp.dot(strip, vectors, precision=highest)  61.4 us
    unnamed x1, blocking collectives  57.8 us
    psum x1, blocking collectives, body(): square_sum = lax.psum(jnp.sum(own_float * own_float), 'dp')  30.5 us
    all_gather x1, blocking collectives, body(): every = lax.all_gather(own_rows, 'dp', axis=0, tiled=True)  24.6 us
  transfers between devices with their start and end apart: 4, of which 4 were waited for; matrix products, arithmetic and copies ran while one was open for 0% of the time, Pallas kernels for 0%

profile of v1, /device:TPU:0, one launch (start us, length us, event | category | flops | bytes accessed | tf_op | source)
XLA Modules:
  0.0 656.1 jit_solution(7291073142813277916)
XLA Ops:
  10.2 2.1 fusion.6
  13.1 2.5 fusion.8
  16.3 2.1 fusion.3
  20.8 24.6 %all-gather.8 = bf16[16,2,8192]{2,1,0:T(2,128)(2,1)S(1)} all-gather(bf16[1,2,8192]{2,1,0:T(2,128)(2,1)S(1)} %reshape.151), channel_id=1, replica_groups=mesh['groups'=2,'dp'=16] {'dp'}, dimensions={0}, use_global_device_ids=true | all-gather | bytes 557056 | tf_op jit(solution)/shard_map/all_gather | solution.py:103
  45.6 30.5 %psum.7 = f32[]{:T(128)} all-reduce(f32[]{:T(128)} %get-tuple-element.10), channel_id=1, replica_groups=mesh['groups'=2,'dp'=16] {'dp'}, use_global_device_ids=true, to_apply=%region_7.8 | all-reduce | flops 1 | bytes 8 | tf_op jit(solution)/shard_map/psum | solution.py:101
  77.7 8.1 %multiply_add_fusion = f32[8192,512]{1,0:T(8,128)S(1)} fusion(f32[8192,512]{1,0:T(8,128)} %param.19, bf16[32,8192]{1,0:T(8,128)(2,1)S(1)} %reshape.152, bf16[32,512]{1,0:T(8,128)(2,1)S(1)} %constant_dynamic-slice_fusion.1, f32[]{:T(128)S(6)} %div.132), kind=kOutput, calls=%fused_computation.2 | convolution fusion | flops 281018368 | bytes 34111492 | tf_op jit(solution)/shard_map/dot_general | solution.py:74
  85.9 5.7 copy-done.1
  91.6 9.1 %fusion.22 = f32[8192,128]{1,0:T(8,128)} fusion(f32[8192,512]{1,0:T(8,128)S(1)} %multiply_add_fusion, bf16[128,512]{0,1:T(8,128)(2,1)S(1)} %copy.13, pred[128]{0:T(512)(128)(4,1)S(1)} %compare_and_fusion), kind=kOutput, calls=%fused_computation.49 | convolution fusion | flops 6442516480 | bytes 21102720 | tf_op jit(solution)/shard_map/dot_general | solution.py:109
  100.7 69.7 %reduce-scatter.5.cloned.1.call-done = f32[512,128]{1,0:T(8,128)} async-done(((f32[8192,128]{1,0:T(8,128)}), f32[512,128]{1,0:T(8,128)}) %reduce-scatter.5.cloned.1.call-update) | async-done | bytes 262160 | tf_op jit(solution)/shard_map/reduce_scatter | solution.py:108
  170.5 1.0 fusion.17
  171.5 19.4 %all-gather.9 = f32[16,1,128]{2,1,0:T(1,128)S(1)} all-gather(f32[1,1,128]{2,1,0:T(1,128)S(1)} %bitcast.65), channel_id=2, replica_groups=mesh['groups'=2,'dp'=16] {'dp'}, dimensions={0}, use_global_device_ids=true | all-gather | bytes 8704 | tf_op jit(solution)/shard_map/all_gather | solution.py:70
  190.8 17.3 %all-gather.10 = f32[16,1,128]{2,1,0:T(1,128)S(1)} all-gather(f32[1,1,128]{2,1,0:T(1,128)S(1)} %bitcast.64), channel_id=3, replica_groups=mesh['groups'=2,'dp'=16] {'dp'}, dimensions={0}, use_global_device_ids=true | all-gather | bytes 8704 | tf_op jit(solution)/shard_map/all_gather | solution.py:70
  208.2 1.0 multiply_reduce_fusion.5
  209.2 18.7 %all-gather.11 = f32[16,1,128]{2,1,0:T(1,128)S(1)} all-gather(f32[1,1,128]{2,1,0:T(1,128)S(1)} %bitcast.67), channel_id=4, replica_groups=mesh['groups'=2,'dp'=16] {'dp'}, dimensions={0}, use_global_device_ids=true | all-gather | bytes 8704 | tf_op jit(solution)/shard_map/all_gather | solution.py:70
  228.0 17.4 %fusion.31 = f32[8192,128]{1,0:T(8,128)} fusion(f32[8192,512]{1,0:T(8,128)} %copy-done.1, f32[512,128]{1,0:T(8,128)} %reduce-scatter.5.cloned.1.call-done, f32[128]{0:T(128)S(1)} %div.134, f32[128]{0:T(128)S(1)} %div.133, bf16[128,512]{0,1:T(8,128)(2,1)S(1)} %copy.13, pred[128]{0:T(512)(128)(4,1)S(1)} %compare_and_fusion), kind=kOutput, calls=%fused_computation.69 | convolution fusion | flops 6442844160 | bytes 21365888 | tf_op jit(solution)/shard_map/dot_general | solution.py:109
  245.5 70.0 %reduce-scatter.7.cloned.1.call-done = f32[512,128]{1,0:T(8,128)} async-done(((f32[8192,128]{1,0:T(8,128)}), f32[512,128]{1,0:T(8,128)}) %reduce-scatter.7.cloned.1.call-update) | async-done | bytes 262160 | tf_op jit(solution)/shard_map/reduce_scatter | solution.py:108
  315.5 1.0 multiply_reduce_fusion.4
  316.5 19.0 %all-gather.12 = f32[16,1,128]{2,1,0:T(1,128)S(1)} all-gather(f32[1,1,128]{2,1,0:T(1,128)S(1)} %bitcast.68), channel_id=5, replica_groups=mesh['groups'=2,'dp'=16] {'dp'}, dimensions={0}, use_global_device_ids=true | all-gather | bytes 8704 | tf_op jit(solution)/shard_map/all_gather | solution.py:70
  335.6 1.0 multiply_reduce_fusion.3
  336.6 17.3 %all-gather.13 = f32[16,1,128]{2,1,0:T(1,128)S(1)} all-gather(f32[1,1,128]{2,1,0:T(1,128)S(1)} %bitcast.63), channel_id=6, replica_groups=mesh['groups'=2,'dp'=16] {'dp'}, dimensions={0}, use_global_device_ids=true | all-gather | bytes 8704 | tf_op jit(solution)/shard_map/all_gather | solution.py:70
  354.0 17.4 %fusion.34 = f32[8192,128]{1,0:T(8,128)} fusion(f32[8192,512]{1,0:T(8,128)} %copy-done.1, f32[512,128]{1,0:T(8,128)S(1)} %multiply_add_fusion.2), kind=kOutput, calls=%fused_computation.71 | convolution fusion | flops 6442450944 | bytes 21233664 | tf_op jit(solution)/shard_map/dot_general | solution.py:109
  371.5 71.1 %reduce-scatter.9.cloned.1.call-done = f32[512,128]{1,0:T(8,128)} async-done(((f32[8192,128]{1,0:T(8,128)}), f32[512,128]{1,0:T(8,128)}) %reduce-scatter.9.cloned.1.call-update) | async-done | bytes 262160 | tf_op jit(solution)/shard_map/reduce_scatter | solution.py:108
  442.6 1.0 multiply_reduce_fusion.2
  443.7 19.2 %all-gather.14 = f32[16,1,128]{2,1,0:T(1,128)S(1)} all-gather(f32[1,1,128]{2,1,0:T(1,128)S(1)} %bitcast.69), channel_id=7, replica_groups=mesh['groups'=2,'dp'=16] {'dp'}, dimensions={0}, use_global_device_ids=true | all-gather | bytes 8704 | tf_op jit(solution)/shard_map/all_gather | solution.py:70
  462.9 1.0 multiply_reduce_fusion.1
  464.0 17.5 %all-gather.15 = f32[16,1,128]{2,1,0:T(1,128)S(1)} all-gather(f32[1,1,128]{2,1,0:T(1,128)S(1)} %bitcast.70), channel_id=8, replica_groups=mesh['groups'=2,'dp'=16] {'dp'}, dimensions={0}, use_global_device_ids=true | all-gather | bytes 8704 | tf_op jit(solution)/shard_map/all_gather | solution.py:70
  481.5 1.0 multiply_add_fusion.1
  482.5 17.4 %fusion.35 = f32[8192,128]{1,0:T(8,128)} fusion(f32[8192,512]{1,0:T(8,128)} %copy-done.1, f32[512,128]{1,0:T(8,128)S(1)} %multiply_add_fusion.1), kind=kOutput, calls=%fused_computation.72 | convolution fusion | flops 6442450944 | bytes 21233664 | tf_op jit(solution)/shard_map/dot_general | solution.py:109
  501.8 68.9 %reduce-scatter.11.cloned.1.call-done = f32[512,128]{1,0:T(8,128)} async-done(((f32[8192,128]{1,0:T(8,128)}), f32[512,128]{1,0:T(8,128)}) %reduce-scatter.11.cloned.1.call-update) | async-done | bytes 262160 | tf_op jit(solution)/shard_map/reduce_scatter | solution.py:108
  570.8 1.0 multiply_reduce_fusion
  571.8 19.1 %all-gather.16 = f32[16,1,128]{2,1,0:T(1,128)S(1)} all-gather(f32[1,1,128]{2,1,0:T(1,128)S(1)} %bitcast.66), channel_id=9, replica_groups=mesh['groups'=2,'dp'=16] {'dp'}, dimensions={0}, use_global_device_ids=true | all-gather | bytes 8704 | tf_op jit(solution)/shard_map/all_gather | solution.py:70
  591.3 57.8 %all-reduce = f32[32,128]{1,0:T(8,128)S(1)} all-reduce(f32[32,128]{1,0:T(8,128)S(1)} %convolution_multiply_fusion), channel_id=14, replica_groups=mesh['groups'=2,'dp'=16] {'dp'}, use_global_device_ids=true, to_apply=%region_26.27.clone | all-reduce | flops 4096 | bytes 32768
  (65 shorter events, 10.7 us)
Async XLA Ops:
  7.2 12.0 %copy-start = (bf16[2,128,4096]{2,1,0:T(8,128)(2,1)S(1)}, bf16[2,128,4096]{2,1,0:T(8,128)(2,1)}, u32[]{:S(2)}) copy-start(bf16[2,128,4096]{2,1,0:T(8,128)(2,1)} %param.10) | copy-start | bytes 6291460
  7.2 9.1 %copy-start.7 = (f32[4096]{0:T(1024)S(1)}, f32[4096]{0:T(1024)}, u32[]{:S(2)}) copy-start(f32[4096]{0:T(1024)} %param.14) | copy-start | bytes 49156
  7.2 8.4 %copy-start.8 = (bf16[4096,14]{0,1:T(8,128)(2,1)S(1)}, bf16[4096,14]{0,1:T(8,128)(2,1)}, u32[]{:S(2)}) copy-start(bf16[4096,14]{0,1:T(8,128)(2,1)} %param.15) | copy-start | bytes 344068
  7.2 8.8 %copy-start.9 = (s32[2]{0:T(128)S(1)}, s32[2]{0:T(128)}, u32[]{:S(2)}) copy-start(s32[2]{0:T(128)} %param.13) | copy-start | bytes 28
  7.2 163.2 %reduce-scatter.5.cloned.1.call-start = ((), (), s32[]{:S(2)}) async-start(), calls=%async_computation.4 | async-start | bytes 4456448 | tf_op jit(solution)/shard_map/reduce_scatter | solution.py:108
  7.3 9.1 %copy-start.3 = (bf16[2,128,4096]{2,1,0:T(8,128)(2,1)S(1)}, bf16[2,128,4096]{2,1,0:T(8,128)(2,1)}, u32[]{:S(2)}) copy-start(bf16[2,128,4096]{2,1,0:T(8,128)(2,1)} %param.11) | copy-start | bytes 6291460
  16.3 2.1 copy-start.4
  16.3 2.8 copy-start.6
  85.8 5.7 copy-start.1
  100.7 214.8 %reduce-scatter.7.cloned.1.call-start = ((), (), s32[]{:S(2)}) async-start(), calls=%async_computation.5 | async-start | bytes 4456448 | tf_op jit(solution)/shard_map/reduce_scatter | solution.py:108
  245.4 70.1 %copy-start.2 = (f32[512,128]{1,0:T(8,128)S(1)}, f32[512,128]{1,0:T(8,128)}, u32[]{:S(2)}) copy-start(f32[512,128]{1,0:T(8,128)} %reduce-scatter.5.cloned.1.call-done) | copy-start | bytes 786436
  245.5 197.2 %reduce-scatter.9.cloned.1.call-start = ((), (), s32[]{:S(2)}) async-start(), calls=%async_computation.6 | async-start | bytes 4456448 | tf_op jit(solution)/shard_map/reduce_scatter | solution.py:108
  371.5 199.3 %reduce-scatter.11.cloned.1.call-start = ((), (), s32[]{:S(2)}) async-start(), calls=%async_computation.7 | async-start | bytes 4456448 | tf_op jit(solution)/shard_map/reduce_scatter | solution.py:108
  499.9 0.7 copy-start.10
  591.0 58.6 %copy-start.5 = (f32[512,128]{1,0:T(8,128)}, f32[512,128]{1,0:T(8,128)S(1)}, u32[]{:S(2)}) copy-start(f32[512,128]{1,0:T(8,128)S(1)} %fusion.20) | copy-start | bytes 786436
Sparse Core Ops, SparseCore 0:
  100.8 69.6 reduce-scatter.4
  245.6 69.8 reduce-scatter.6
  371.6 71.0 reduce-scatter.8
  500.1 70.6 reduce-scatter.10
